TPU v7x, 32 devices: a whole 2x2x4 slice. The times are simulated.
32 devices in a mesh: dp: 2 (over y), row: 4 (over z), col: 4 (over x, core).
Axes of the slice: x: 2, y: 2, z: 4, core: 2. Of those that a mesh axis runs over, the one named last changes fastest.
Arguments:
- inputs: bfloat16 [18464, 1024], P(('dp', 'row'), 'col'), may hold values from -30 to 30
- query_weight: bfloat16 [1024, 1024], P('row', 'col'), may hold values from -7 to 7
- key_weight: bfloat16 [1024, 1024], P('row', 'col'), may hold values from -7 to 7
- value_weight: bfloat16 [1024, 1024], P('row', 'col'), may hold values from -0.1875 to 0.1875
- query_bias: float32 [1024], P('col'), may hold values from -3 to 3
- value_bias: float32 [1024], P('col'), may hold values from -0.3 to 0.3
- out_weight: bfloat16 [1024, 1024], P('col', 'row'), may hold values from -1.5 to 1.5
- out_bias: float32 [1024], P('col'), may hold values from -3 to 3
- up_weight: bfloat16 [1024, 4096], P('row', 'col'), may hold values from -0.1875 to 0.1875
- up_bias: float32 [4096], P('col'), may hold values from -3 to 3
- down_weight: bfloat16 [4096, 1024], P('col', 'row'), may hold values from -0.09375 to 0.09375
- down_bias: float32 [1024], P('col'), may hold values from -3 to 3
- first_gain: float32 [1024], P('col'), may hold values from 0.1 to 1.9
- first_shift: float32 [1024], P('col'), may hold values from -2 to 2
- second_gain: float32 [1024], P('col'), may hold values from 0.1 to 1.9
- second_shift: float32 [1024], P('col'), may hold values from -2 to 2
- cotangent: bfloat16 [18464, 1024], P(('dp', 'row'), 'col'), may hold values from -6 to 6
Outputs:
- outputs: bfloat16 [18464, 1024], P(('dp', 'row'), 'col')
- input_grad: float32 [18464, 1024], P(('dp', 'row'), 'col')
- query_weight_grad: float32 [1024, 1024], P('row', 'col')
- key_weight_grad: float32 [1024, 1024], P('row', 'col')
- value_weight_grad: float32 [1024, 1024], P('row', 'col')
- query_bias_grad: float32 [1024], P('col')
- value_bias_grad: float32 [1024], P('col')
- out_weight_grad: float32 [1024, 1024], P('col', 'row')
- out_bias_grad: float32 [1024], P('col')
- up_weight_grad: float32 [1024, 4096], P('row', 'col')
- up_bias_grad: float32 [4096], P('col')
- down_weight_grad: float32 [4096, 1024], P('col', 'row')
- down_bias_grad: float32 [1024], P('col')
- first_gain_grad: float32 [1024], P('col')
- first_shift_grad: float32 [1024], P('col')
- second_gain_grad: float32 [1024], P('col')
- second_shift_grad: float32 [1024], P('col')
All inputs are finite; a program needn't handle non-finite values.
Results may differ from a plain program's by a relative error of at most 0.012.
The roundings to bfloat16 on the way count: a program that leaves them out, or rounds other values in their place, can miss the bound.
Values may be sent and summed in bfloat16 or wider, within the bound.
No kernel may reach another device: no remote copies, remote signals or barrier semaphores. Data moves between devices by JAX's collectives and lax.ppermute only.
A program may use at most 192 MiB of HBM per device.

v0:
```python
import jax
import jax.numpy as jnp
from jax import lax
from jax.sharding import PartitionSpec as P

D = 1024
HD = 64
SEQ = 577


def matmul(left_side, right_side):
    return jnp.dot(left_side, right_side, preferred_element_type=jnp.float32)


def matmul_tn(left_side, right_side):
    return lax.dot_general(
        left_side, right_side, (((0,), (0,)), ((), ())), preferred_element_type=jnp.float32
    )


def matmul_nt(left_side, right_side):
    return lax.dot_general(
        left_side, right_side, (((1,), (1,)), ((), ())), preferred_element_type=jnp.float32
    )


def feature_totals(first, second):
    return lax.psum(
        (jnp.sum(first, axis=1, keepdims=True), jnp.sum(second, axis=1, keepdims=True)), "col"
    )


def gather_normed(values):
    return lax.all_gather(values, "col", axis=1, tiled=True)


def gather_grads(values):
    return lax.all_gather(values, "col", axis=1, tiled=True)


def scatter_partial(values):
    return lax.psum_scatter(values, "col", scatter_dimension=1, tiled=True)


def norm_forward(inputs_rows, gain_vector, shift_vector):
    row_total, squares = feature_totals(inputs_rows, inputs_rows * inputs_rows)
    middle = row_total / D
    spread = squares / D - middle * middle
    scaled = lax.rsqrt(spread + 1e-06)
    centred = (inputs_rows - middle) * scaled
    return (centred * gain_vector + shift_vector, centred, scaled)


def norm_backward(upstream, gain_vector, centred, scaled):
    dcentred = upstream * gain_vector
    first, second = feature_totals(dcentred, dcentred * centred)
    return scaled * (dcentred - first / D - centred * second / D)


def attend_image(operands):
    query_rows, key_rows, value_rows = operands
    scores = (
        jnp.einsum("qhd,khd->hqk", query_rows, key_rows, preferred_element_type=jnp.float32) * 0.125
    )
    row_peak = jnp.max(scores, axis=-1, keepdims=True)
    exponent = jnp.exp(scores - row_peak)
    row_total = jnp.sum(exponent, axis=-1, keepdims=True)
    soft_weights = (exponent / row_total).astype(jnp.bfloat16)
    mixed_rows = jnp.einsum(
        "hqk,khd->qhd", soft_weights, value_rows, preferred_element_type=jnp.float32
    )
    return (mixed_rows.astype(jnp.bfloat16), row_peak + jnp.log(row_total))


def attend_back(operands):
    query_rows, key_rows, value_rows, grad_rows, logsum = operands
    scores = (
        jnp.einsum("qhd,khd->hqk", query_rows, key_rows, preferred_element_type=jnp.float32) * 0.125
    )
    soft_weights = jnp.exp(scores - logsum)
    dprobs = jnp.einsum("qhd,khd->hqk", grad_rows, value_rows, preferred_element_type=jnp.float32)
    dvalues = jnp.einsum(
        "hqk,qhd->khd",
        soft_weights.astype(jnp.bfloat16),
        grad_rows,
        preferred_element_type=jnp.float32,
    )
    row_dot = jnp.sum(soft_weights * dprobs, axis=-1, keepdims=True)
    dscores = (soft_weights * (dprobs - row_dot)).astype(jnp.bfloat16)
    dqueries = (
        jnp.einsum("hqk,khd->qhd", dscores, key_rows, preferred_element_type=jnp.float32) * 0.125
    )
    key_grads = (
        jnp.einsum("hqk,qhd->khd", dscores, query_rows, preferred_element_type=jnp.float32) * 0.125
    )
    return (
        dqueries.astype(jnp.bfloat16),
        key_grads.astype(jnp.bfloat16),
        dvalues.astype(jnp.bfloat16),
    )


def gelu_exact(values):
    return jax.nn.gelu(values, approximate=False)


def local(
    inputs,
    query_weight,
    key_weight,
    value_weight,
    query_bias,
    value_bias,
    out_weight,
    out_bias,
    up_weight,
    up_bias,
    down_weight,
    down_bias,
    first_gain,
    first_shift,
    second_gain,
    second_shift,
    cotangent,
):
    tokens_here = inputs.shape[0]
    feature_width = inputs.shape[1]
    images = tokens_here // SEQ
    heads_here = feature_width // HD
    head_shape = (images, SEQ, heads_here, HD)
    residual = inputs.astype(jnp.float32)
    query_full, key_full, value_full, out_full, up_full, down_full = (
        lax.all_gather(query_weight, "row", axis=0, tiled=True),
        lax.all_gather(key_weight, "row", axis=0, tiled=True),
        lax.all_gather(value_weight, "row", axis=0, tiled=True),
        lax.all_gather(out_weight, "row", axis=1, tiled=True),
        lax.all_gather(up_weight, "row", axis=0, tiled=True),
        lax.all_gather(down_weight, "row", axis=1, tiled=True),
    )
    normed_one, centred_one, scaled_one = norm_forward(residual, first_gain, first_shift)
    wide_one = gather_normed(normed_one.astype(jnp.bfloat16))
    queries = (matmul(wide_one, query_full) + query_bias).astype(jnp.bfloat16)
    key_rows = matmul(wide_one, key_full).astype(jnp.bfloat16)
    values = (matmul(wide_one, value_full) + value_bias).astype(jnp.bfloat16)
    query_heads = queries.reshape(head_shape)
    key_heads = key_rows.reshape(head_shape)
    value_heads = values.reshape(head_shape)
    attended, logsums = lax.map(attend_image, (query_heads, key_heads, value_heads))
    attended = attended.reshape(tokens_here, feature_width)
    branch_attn = (
        lax.psum_scatter(matmul(attended, out_full), "col", scatter_dimension=1, tiled=True)
        + out_bias
    )
    middle_sum = residual + branch_attn
    normed_two, centred_two, scaled_two = norm_forward(middle_sum, second_gain, second_shift)
    wide_two = gather_normed(normed_two.astype(jnp.bfloat16))
    up_values = matmul(wide_two, up_full) + up_bias
    gelu_value, gelu_back = jax.vjp(gelu_exact, up_values)
    hidden = gelu_value.astype(jnp.bfloat16)
    branch_mlp = (
        lax.psum_scatter(
            matmul(hidden, down_full).astype(jnp.bfloat16), "col", scatter_dimension=1, tiled=True
        ).astype(jnp.float32)
        + down_bias
    )
    outputs = (middle_sum + branch_mlp).astype(jnp.bfloat16)
    grad_top = cotangent.astype(jnp.float32)
    down_bias_grad = jnp.sum(grad_top, axis=0)
    wide_grad = gather_grads(cotangent)
    down_grad_full = matmul_tn(hidden, wide_grad)
    hidden_grad = matmul_nt(wide_grad, down_full)
    pre_grad = gelu_back(hidden_grad)[0].astype(jnp.bfloat16)
    up_bias_grad = jnp.sum(pre_grad.astype(jnp.float32), axis=0)
    up_grad_full = matmul_tn(wide_two, pre_grad)
    normed_grad_two = scatter_partial(matmul_nt(pre_grad, up_full))
    second_gain_grad = jnp.sum(normed_grad_two * centred_two, axis=0)
    second_shift_grad = jnp.sum(normed_grad_two, axis=0)
    middle_grad = grad_top + norm_backward(normed_grad_two, second_gain, centred_two, scaled_two)
    attn_grad = middle_grad.astype(jnp.bfloat16)
    out_bias_grad = jnp.sum(attn_grad.astype(jnp.float32), axis=0)
    wide_attn_grad = gather_grads(attn_grad)
    out_grad_full = matmul_tn(attended, wide_attn_grad)
    head_grad = matmul_nt(wide_attn_grad, out_full).astype(jnp.bfloat16)
    dqueries, key_grads, dvalues = lax.map(
        attend_back, (query_heads, key_heads, value_heads, head_grad.reshape(head_shape), logsums)
    )
    dqueries = dqueries.reshape(tokens_here, feature_width)
    key_grads = key_grads.reshape(tokens_here, feature_width)
    dvalues = dvalues.reshape(tokens_here, feature_width)
    query_bias_grad = jnp.sum(dqueries.astype(jnp.float32), axis=0)
    value_bias_grad = jnp.sum(dvalues.astype(jnp.float32), axis=0)
    query_grad_full = matmul_tn(wide_one, dqueries)
    key_grad_full = matmul_tn(wide_one, key_grads)
    value_grad_full = matmul_tn(wide_one, dvalues)
    partial_one = (
        matmul_nt(dqueries, query_full)
        + matmul_nt(key_grads, key_full)
        + matmul_nt(dvalues, value_full)
    )
    normed_grad_one = scatter_partial(partial_one)
    first_gain_grad = jnp.sum(normed_grad_one * centred_one, axis=0)
    first_shift_grad = jnp.sum(normed_grad_one, axis=0)
    input_grad = middle_grad + norm_backward(normed_grad_one, first_gain, centred_one, scaled_one)
    vectors = jnp.concatenate(
        [
            query_bias_grad,
            value_bias_grad,
            out_bias_grad,
            down_bias_grad,
            first_gain_grad,
            first_shift_grad,
            second_gain_grad,
            second_shift_grad,
            up_bias_grad,
        ]
    )
    summed = lax.psum(
        (
            query_grad_full,
            key_grad_full,
            value_grad_full,
            out_grad_full,
            up_grad_full,
            down_grad_full,
            vectors,
        ),
        ("dp", "row"),
    )
    row_index = lax.axis_index("row")
    query_grad = lax.dynamic_slice_in_dim(
        summed[0], row_index * query_weight.shape[0], query_weight.shape[0], 0
    )
    key_grad = lax.dynamic_slice_in_dim(
        summed[1], row_index * key_weight.shape[0], key_weight.shape[0], 0
    )
    value_grad = lax.dynamic_slice_in_dim(
        summed[2], row_index * value_weight.shape[0], value_weight.shape[0], 0
    )
    out_grad = lax.dynamic_slice_in_dim(
        summed[3], row_index * out_weight.shape[1], out_weight.shape[1], 1
    )
    up_grad = lax.dynamic_slice_in_dim(
        summed[4], row_index * up_weight.shape[0], up_weight.shape[0], 0
    )
    down_grad = lax.dynamic_slice_in_dim(
        summed[5], row_index * down_weight.shape[1], down_weight.shape[1], 1
    )
    vector_sums = summed[6]
    pieces = [
        vector_sums[feature_width * place : feature_width * (place + 1)] for place in range(8)
    ]
    up_bias_sum = vector_sums[8 * feature_width :]
    return (
        outputs,
        input_grad,
        query_grad,
        key_grad,
        value_grad,
        pieces[0],
        pieces[1],
        out_grad,
        pieces[2],
        up_grad,
        up_bias_sum,
        down_grad,
        pieces[3],
        pieces[4],
        pieces[5],
        pieces[6],
        pieces[7],
    )


def solution(mesh):
    in_specs = (
        P(("dp", "row"), "col"),
        P("row", "col"),
        P("row", "col"),
        P("row", "col"),
        P("col"),
        P("col"),
        P("col", "row"),
        P("col"),
        P("row", "col"),
        P("col"),
        P("col", "row"),
        P("col"),
        P("col"),
        P("col"),
        P("col"),
        P("col"),
        P(("dp", "row"), "col"),
    )
    out_specs = (
        P(("dp", "row"), "col"),
        P(("dp", "row"), "col"),
        P("row", "col"),
        P("row", "col"),
        P("row", "col"),
        P("col"),
        P("col"),
        P("col", "row"),
        P("col"),
        P("row", "col"),
        P("col"),
        P("col", "row"),
        P("col"),
        P("col"),
        P("col"),
        P("col"),
        P("col"),
    )
    return jax.shard_map(local, mesh=mesh, in_specs=in_specs, out_specs=out_specs, check_vma=False)
```

profile of v0, /device:TPU:0, one launch (start us, length us, event | category | flops | bytes accessed | tf_op | source)
XLA Modules:
  0.0 1243.2 jit_solution(17970794028962596964)
XLA Ops:
  10.2 12.9 %all-reduce.4 = (f32[2308,1]{0,1:T(1,128)S(1)}, f32[2308,1]{0,1:T(1,128)S(1)}) all-reduce(f32[2308,1]{0,1:T(1,128)S(1)} %broadcast_in_dim.57, f32[2308,1]{0,1:T(1,128)S(1)} %broadcast_in_dim.58), channel_id=1, replica_groups=mesh['dp'=2,'row'=4,'col'=4] {'col'}, use_global_device_ids=true, to_apply=%region_1.0 | all-reduce | flops 4616 | bytes 36928 | tf_op jit(solution)/shard_map/psum | solution.py:28
  27.2 15.0 %all_gather.31 = bf16[1024,256]{1,0:T(8,128)(2,1)S(1)} all-gather(bf16[256,256]{1,0:T(8,128)(2,1)S(1)} %copy-done.27), channel_id=1, replica_groups=mesh['dp'=2,'row'=4,'col'=4] {'row'}, dimensions={0}, use_global_device_ids=true | all-gather | bytes 655360 | tf_op jit(solution)/shard_map/all_gather | solution.py:135
  42.2 17.4 %all_gather.32 = bf16[1024,256]{1,0:T(8,128)(2,1)S(1)} all-gather(bf16[256,256]{1,0:T(8,128)(2,1)S(1)} %copy-done.28), channel_id=1, replica_groups=mesh['dp'=2,'row'=4,'col'=4] {'row'}, dimensions={0}, use_global_device_ids=true | all-gather | bytes 655360 | tf_op jit(solution)/shard_map/all_gather | solution.py:133
  59.7 14.8 %all_gather.33 = bf16[1024,256]{1,0:T(8,128)(2,1)S(1)} all-gather(bf16[256,256]{1,0:T(8,128)(2,1)S(1)} %copy-done.29), channel_id=1, replica_groups=mesh['dp'=2,'row'=4,'col'=4] {'row'}, dimensions={0}, use_global_device_ids=true | all-gather | bytes 655360 | tf_op jit(solution)/shard_map/all_gather | solution.py:134
  74.5 15.8 %all_gather.34 = bf16[256,1024]{1,0:T(8,128)(2,1)} all-gather(bf16[256,256]{1,0:T(8,128)(2,1)S(1)} %copy-done.30), channel_id=1, replica_groups=mesh['dp'=2,'row'=4,'col'=4] {'row'}, dimensions={1}, use_global_device_ids=true | all-gather | bytes 655360 | tf_op jit(solution)/shard_map/all_gather | solution.py:136
  121.4 23.7 %while.26 = (s32[]{:T(128)}, bf16[4,577,4,64]{1,3,2,0:T(8,128)(2,1)}, f32[4,4,577,1]{2,1,3,0:T(4,128)}, bf16[4,577,4,64]{1,3,2,0:T(8,128)(2,1)}, bf16[4,577,4,64...) while((s32[]{:T(128)}, bf16[4,577,4,64]{1,3,2,0:T(8,128)(2,1)}, ...), condition=%wide.region_7.8_spmd, body=%wide.region_4.7_spmd.sunk | while | flops 353050112 | bytes 17368812 | solution.py:148
  149.5 14.1 %reshape.96 = bf16[2308,256]{0,1:T(8,128)(2,1)} reshape(bf16[4,577,4,64]{1,0,3,2:T(4,128)(2,1)} %copy.55) | data formatting | bytes 2363392 | tf_op jit(solution)/shard_map/reshape | solution.py:149
  163.7 6.3 fusion.82
  170.7 78.4 %reduce-scatter.5.cloned.1.call-done = f32[2308,256]{1,0:T(8,128)} async-done(((f32[2308,1024]{1,0:T(8,128)}), f32[2308,256]{1,0:T(8,128)}) %reduce-scatter.5.cloned.1.call-update) | async-done | bytes 2363408 | tf_op jit(solution)/shard_map/reduce_scatter | solution.py:151
  251.6 10.2 all-reduce.3
  266.8 37.3 %all-gather.9.cloned.1.call-done = bf16[2308,1024]{1,0:T(8,128)(2,1)} async-done(((bf16[2308,256]{1,0:T(8,128)(2,1)}), bf16[2308,1024]{1,0:T(8,128)(2,1)}) %all-gather.9.cloned.1.call-update) | async-done | bytes 4726800 | tf_op jit(solution)/shard_map/all_gather | solution.py:34
  304.0 10.1 fusion.83
  314.2 37.5 %all-gather.13.cloned.1.call-done = bf16[1024,1024]{1,0:T(8,128)(2,1)} async-done(((bf16[1024,256]{1,0:T(8,128)(2,1)}), bf16[1024,1024]{1,0:T(8,128)(2,1)}) %all-gather.13.cloned.1.call-update) | async-done | bytes 2097168 | tf_op jit(solution)/shard_map/all_gather | solution.py:138
  351.6 37.8 %all-gather.15.cloned.1.call-done = bf16[2308,1024]{1,0:T(8,128)(2,1)} async-done(((bf16[2308,256]{1,0:T(8,128)(2,1)}), bf16[2308,1024]{1,0:T(8,128)(2,1)}) %all-gather.15.cloned.1.call-update) | async-done | bytes 4726800 | tf_op jit(solution)/shard_map/all_gather | solution.py:38
  389.4 32.0 %convert_reduce_fusion = (f32[1024]{0:T(1024)}, bf16[2308,1024]{1,0:T(8,128)(2,1)S(1)}, f32[2308,1024]{1,0:T(8,128)}) fusion(f32[2308,1024]{1,0:T(8,128)} %fusion.83, f32[1024]{0:T(1024)S(1)} %copy-done.36, bf16[2308,1024]{1,0:T(8,128)(2,1)} %all-gather.15.cloned.1.call-done, bf16[1024,1024]{1,0:T(8,128)(2,1)} %all-gather.13.cloned.1.call-done), kind=kOutput, calls=%fused_computation.62 | convolution fusion | flops 5017480192 | bytes 30466048 | tf_op jit(solution)/shard_map/dot_general | solution.py:22
  423.6 8.0 fusion.84
  432.1 13.0 %multiply_convert_fusion.1 = bf16[2308,1024]{1,0:T(8,128)(2,1)} fusion(f32[2308,1024]{1,0:T(8,128)} %get-tuple-element.196, f32[2308,1024]{1,0:T(8,128)} %fusion.83, f32[1024]{0:T(1024)S(1)} %copy-done.36), kind=kLoop, calls=%fused_computation.65 | loop fusion | flops 9453568 | bytes 23638016 | tf_op jit(solution)/shard_map/convert_element_type | solution.py:159
  445.1 10.0 convolution_convert_fusion
  455.2 54.5 %reduce-scatter.9.cloned.1.call-done = f32[2308,256]{1,0:T(8,128)} async-done(((f32[2308,1024]{1,0:T(8,128)}), f32[2308,256]{1,0:T(8,128)}) %reduce-scatter.9.cloned.1.call-update) | async-done | bytes 2363408 | tf_op jit(solution)/shard_map/reduce_scatter | solution.py:42
  513.9 11.4 all-reduce.2
  526.7 33.3 %reduce-scatter.7.cloned.1.call-done = bf16[2308,256]{1,0:T(8,128)(2,1)} async-done(((bf16[2308,1024]{1,0:T(8,128)(2,1)}), bf16[2308,256]{1,0:T(8,128)(2,1)}) %reduce-scatter.7.cloned.1.call-update) | async-done | bytes 1181712 | tf_op jit(solution)/shard_map/reduce_scatter | solution.py:161
  560.1 6.5 convert_reduce_fusion.5
  566.6 10.4 fusion.91
  577.1 8.9 fusion.92
  586.0 18.8 %all-gather.17.cloned.1.call-done = bf16[2308,1024]{1,0:T(8,128)(2,1)} async-done(((bf16[2308,256]{1,0:T(8,128)(2,1)}), bf16[2308,1024]{1,0:T(8,128)(2,1)}) %all-gather.17.cloned.1.call-update) | async-done | bytes 4726800 | tf_op jit(solution)/shard_map/all_gather | solution.py:38
  619.2 43.5 %while.27 = (s32[]{:T(128)}, bf16[4,577,4,64]{1,3,2,0:T(8,128)(2,1)}, bf16[4,577,4,64]{1,3,2,0:T(8,128)(2,1)}, bf16[4,577,4,64]{1,3,2,0:T(8,128)(2,1)}, bf16[4,5...) while((s32[]{:T(128)}, ...), condition=%wide.region_21.22_spmd, body=%wide.region_19.21_spmd.sunk | while | flops 869015040 | bytes 49986844 | solution.py:184
  682.1 5.2 fusion.87
  697.5 5.1 add_add_fusion
  709.8 378.3 %all-reduce.7.cloned.1.call-done = (f32[1024,256]{1,0:T(8,128)}, f32[1024,256]{1,0:T(8,128)}, f32[1024,256]{1,0:T(8,128)}, f32[256,1024]{1,0:T(8,128)}, f32[1024,1024]{1,0:T(8,128)}, /*index=5*/f32[1024,1024]{1,0:T(8,128)}) async-done(((f32[1024,256]{1,0:T(8,128)}, f32[1024,256]{1,0:T(8,128)}, f32[1024,256]{1,0:T(8,128)}, f32[256,1024]{1,0:T(8,128)}, f32[1024,1024]{1,0:T(8,128)}, ...) | async-done | bytes 12582928 | tf_op jit(solution)/shard_map/psum | solution.py:217
  1097.0 70.7 %reduce-scatter.11.cloned.1.call-done = f32[2308,256]{1,0:T(8,128)} async-done(((f32[2308,1024]{1,0:T(8,128)}), f32[2308,256]{1,0:T(8,128)}) %reduce-scatter.11.cloned.1.call-update) | async-done | bytes 2363408 | tf_op jit(solution)/shard_map/reduce_scatter | solution.py:42
  1177.2 37.3 %psum.116 = f32[3072]{0:T(1024)} all-reduce(f32[3072]{0:T(1024)} %constant_dynamic-update-slice_fusion), channel_id=1, replica_groups=mesh['dp'=2,'row'=4,'col'=4] {'dp','row'}, use_global_device_ids=true, to_apply=%region_39.40 | all-reduce | flops 3072 | bytes 24576 | tf_op jit(solution)/shard_map/psum | solution.py:217
  1218.4 11.6 all-reduce.1
  (231 shorter events, 203.9 us)
Async XLA Ops:
  8.0 19.1 %copy-start.27 = (bf16[256,256]{1,0:T(8,128)(2,1)S(1)}, bf16[256,256]{1,0:T(8,128)(2,1)}, u32[]{:S(2)}) copy-start(bf16[256,256]{1,0:T(8,128)(2,1)} %param.24) | copy-start | bytes 393220
  8.0 34.2 %copy-start.28 = (bf16[256,256]{1,0:T(8,128)(2,1)S(1)}, bf16[256,256]{1,0:T(8,128)(2,1)}, u32[]{:S(2)}) copy-start(bf16[256,256]{1,0:T(8,128)(2,1)} %param.22) | copy-start | bytes 393220
  8.0 51.6 %copy-start.29 = (bf16[256,256]{1,0:T(8,128)(2,1)S(1)}, bf16[256,256]{1,0:T(8,128)(2,1)}, u32[]{:S(2)}) copy-start(bf16[256,256]{1,0:T(8,128)(2,1)} %param.23) | copy-start | bytes 393220
  8.1 82.2 %all-gather.7.cloned.1.call-start = ((), (), s32[]{:S(2)}) async-start(), calls=%async_computation.4 | async-start | bytes 5918720 | tf_op jit(solution)/shard_map/all_gather | solution.py:34
  10.2 64.3 %copy-start.30 = (bf16[256,256]{1,0:T(8,128)(2,1)S(1)}, bf16[256,256]{1,0:T(8,128)(2,1)}, u32[]{:S(2)}) copy-start(bf16[256,256]{1,0:T(8,128)(2,1)} %param.27) | copy-start | bytes 393220
  23.9 66.4 %copy-start.38 = (f32[256]{0:T(256)S(1)}, f32[256]{0:T(256)}, u32[]{:S(2)}) copy-start(f32[256]{0:T(256)} %param.26) | copy-start | bytes 3076
  27.1 222.0 %reduce-scatter.5.cloned.1.call-start = ((), (), s32[]{:S(2)}) async-start(), calls=%async_computation.5 | async-start | bytes 11837440 | tf_op jit(solution)/shard_map/reduce_scatter | solution.py:151
  42.2 48.0 %copy-start.16 = (bf16[1024,256]{1,0:T(8,128)(2,1)}, bf16[1024,256]{1,0:T(8,128)(2,1)S(1)}, u32[]{:S(2)}) copy-start(bf16[1024,256]{1,0:T(8,128)(2,1)S(1)} %all_gather.31) | copy-start | bytes 1572868
  59.7 41.9 %copy-start.18 = (bf16[1024,256]{1,0:T(8,128)(2,1)}, bf16[1024,256]{1,0:T(8,128)(2,1)S(1)}, u32[]{:S(2)}) copy-start(bf16[1024,256]{1,0:T(8,128)(2,1)S(1)} %all_gather.32) | copy-start | bytes 1572868
  74.5 36.4 %copy-start.20 = (bf16[1024,256]{1,0:T(8,128)(2,1)}, bf16[1024,256]{1,0:T(8,128)(2,1)S(1)}, u32[]{:S(2)}) copy-start(bf16[1024,256]{1,0:T(8,128)(2,1)S(1)} %all_gather.33) | copy-start | bytes 1572868
  145.2 24.9 %copy-start.2 = (bf16[4,577,4,64]{1,3,2,0:T(8,128)(2,1)}, bf16[4,577,4,64]{1,3,2,0:T(8,128)(2,1)S(1)}, u32[]{:S(2)}) copy-start(bf16[4,577,4,64]{1,3,2,0:T(8,128)(2,1)S(1)} %get-tuple-element.398) | copy-start | bytes 3545092
  145.2 24.9 %copy-start.4 = (bf16[4,577,4,64]{1,3,2,0:T(8,128)(2,1)}, bf16[4,577,4,64]{1,3,2,0:T(8,128)(2,1)S(1)}, u32[]{:S(2)}) copy-start(bf16[4,577,4,64]{1,3,2,0:T(8,128)(2,1)S(1)} %get-tuple-element.399) | copy-start | bytes 3545092
  145.2 18.5 %copy-start.21 = (bf16[256,1024]{1,0:T(8,128)(2,1)S(1)}, bf16[256,1024]{1,0:T(8,128)(2,1)}, u32[]{:S(2)}) copy-start(bf16[256,1024]{1,0:T(8,128)(2,1)} %all_gather.34) | copy-start | bytes 1572868
  170.0 79.1 %copy-start = (bf16[2308,256]{1,0:T(8,128)(2,1)S(1)}, bf16[2308,256]{1,0:T(8,128)(2,1)}, u32[]{:S(2)}) copy-start(bf16[2308,256]{1,0:T(8,128)(2,1)} %param.21) | copy-start | bytes 3545092
  170.1 96.7 %all-gather.11.cloned.1.call-start = ((), (), s32[]{:S(2)}) async-start(), calls=%async_computation.7 | async-start | bytes 2621440 | tf_op jit(solution)/shard_map/all_gather | solution.py:137
  170.6 91.9 %copy-start.32 = (f32[256]{0:T(256)S(1)}, f32[256]{0:T(256)}, u32[]{:S(2)}) copy-start(f32[256]{0:T(256)} %param.35) | copy-start | bytes 3076
  170.6 133.4 %all-gather.9.cloned.1.call-start = ((), (), s32[]{:S(2)}) async-start(), calls=%async_computation.6 | async-start | bytes 5918720 | tf_op jit(solution)/shard_map/all_gather | solution.py:34
  265.4 86.3 %all-gather.13.cloned.1.call-start = ((), (), s32[]{:S(2)}) async-start(), calls=%async_computation.8 | async-start | bytes 2621440 | tf_op jit(solution)/shard_map/all_gather | solution.py:138
  266.0 123.5 %all-gather.15.cloned.1.call-start = ((), (), s32[]{:S(2)}) async-start(), calls=%async_computation.10 | async-start | bytes 5918720 | tf_op jit(solution)/shard_map/all_gather | solution.py:38
  266.7 122.7 %copy-start.36 = (f32[1024]{0:T(1024)S(1)}, f32[1024]{0:T(1024)}, u32[]{:S(2)}) copy-start(f32[1024]{0:T(1024)} %param.30) | copy-start | bytes 12292
  266.7 243.0 %reduce-scatter.9.cloned.1.call-start = ((), (), s32[]{:S(2)}) async-start(), calls=%async_computation.11 | async-start | bytes 11837440 | tf_op jit(solution)/shard_map/reduce_scatter | solution.py:42
  389.4 34.2 %copy-start.37 = (bf16[1024,1024]{1,0:T(8,128)(2,1)S(1)}, bf16[1024,1024]{1,0:T(8,128)(2,1)}, u32[]{:S(2)}) copy-start(bf16[1024,1024]{1,0:T(8,128)(2,1)} %all-gather.11.cloned.1.call-done) | copy-start | bytes 6291460
  431.7 128.4 %reduce-scatter.7.cloned.1.call-start = ((), (), s32[]{:S(2)}) async-start(), calls=%async_computation.9 | async-start | bytes 5918720 | tf_op jit(solution)/shard_map/reduce_scatter | solution.py:161
  455.1 104.9 %copy-start.15 = (bf16[2308,256]{1,0:T(8,128)(2,1)S(1)}, bf16[2308,256]{1,0:T(8,128)(2,1)}, u32[]{:S(2)}) copy-start(bf16[2308,256]{1,0:T(8,128)(2,1)} %param.37) | copy-start | bytes 3545092
  455.2 149.7 %all-gather.17.cloned.1.call-start = ((), (), s32[]{:S(2)}) async-start(), calls=%async_computation.12 | async-start | bytes 5918720 | tf_op jit(solution)/shard_map/all_gather | solution.py:38
  566.6 10.5 slice-start
  566.6 521.6 %all-reduce.7.cloned.1.call-start = ((), (), s32[]{:S(2)}) async-start(), calls=%async_computation.14 | async-start | bytes 25165824 | tf_op jit(solution)/shard_map/psum | solution.py:217
  577.1 27.8 %copy-start.22 = (bf16[256,1024]{1,0:T(8,128)(2,1)S(1)}, bf16[256,1024]{1,0:T(8,128)(2,1)}, u32[]{:S(2)}) copy-start(bf16[256,1024]{1,0:T(8,128)(2,1)} %all_gather.34) | copy-start | bytes 1572868
  693.0 474.7 %reduce-scatter.11.cloned.1.call-start = ((), (), s32[]{:S(2)}) async-start(), calls=%async_computation.13 | async-start | bytes 11837440 | tf_op jit(solution)/shard_map/reduce_scatter | solution.py:42
  1088.2 79.5 %copy-start.1 = (bf16[2308,256]{1,0:T(8,128)(2,1)S(1)}, bf16[2308,256]{1,0:T(8,128)(2,1)}, u32[]{:S(2)}) copy-start(bf16[2308,256]{1,0:T(8,128)(2,1)} %param.21) | copy-start | bytes 3545092
  1088.2 79.5 %copy-start.31 = (f32[256]{0:T(256)S(1)}, f32[256]{0:T(256)}, u32[]{:S(2)}) copy-start(f32[256]{0:T(256)} %param.33) | copy-start | bytes 3076
  1094.2 136.6 %copy-start.8 = (f32[2308,256]{1,0:T(8,128)S(1)}, f32[2308,256]{1,0:T(8,128)}, u32[]{:S(2)}) copy-start(f32[2308,256]{1,0:T(8,128)} %get-tuple-element.199) | copy-start | bytes 7090180
  (27 other events, 113.4 us)
Sparse Core Ops, SparseCore 0:
  27.2 38.4 all-gather.6
  170.2 78.9 reduce-scatter.4
  566.7 38.1 all-gather.16
  693.1 395.0 all-reduce.6
  1090.6 77.0 reduce-scatter.10
Sparse Core Ops, SparseCore 1:
  172.1 46.4 all-gather.10
  265.5 38.5 all-gather.8
  305.5 46.1 all-gather.12
  353.2 36.2 all-gather.14
  431.8 77.8 reduce-scatter.8
  512.2 47.8 reduce-scatter.6
where the time goes:
time: 1250 us; the launch traced here: 1240 us
  waiting for transfers between devices  749 us (60%)
  matrix products  179 us (14%)
  blocking collectives  147 us (12%)
  local copies, waits for them, and re-layouts  93.2 us (7%)
  other arithmetic  58.6 us (5%)
  between operations  16.1 us (1%)
    psum x1, waiting for transfers between devices, local(): lax.psum((query_grad_full, key_grad_full, value_grad_full, out_grad_full,...  378 us
    reduce_scatter x2, waiting for transfers between devices, scatter_partial(): return lax.psum_scatter(values, 'col', scatter_dimension=1, tiled=True)  125 us
    reduce_scatter x1, waiting for transfers between devices, local(): lax.psum_scatter(matmul(attended, out_full), 'col', scatter_dimension=1,...  78.4 us
    all_gather x2, waiting for transfers between devices, gather_grads(): return lax.all_gather(values, 'col', axis=1, tiled=True)  56.6 us
    dot_general x6, matrix products, matmul_nt(): lax.dot_general(left_side, right_side, (((1,), (1,)), ((), ())), preferre...  53.1 us
    psum x4, blocking collectives, feature_totals(): lax.psum((jnp.sum(first, axis=1, keepdims=True), jnp.sum(second, axis=1,...  46.3 us
    dot_general x6, matrix products, matmul(): return jnp.dot(left_side, right_side, preferred_element_type=jnp.float32)  38.7 us
    all_gather x1, waiting for transfers between devices, local(): lax.all_gather(down_weight, 'row', axis=1, tiled=True)  37.5 us
  transfers between devices with their start and end apart: 11, of which 9 were waited for; matrix products, arithmetic and copies ran while one was open for 7% of the time, Pallas kernels for 0%

commit v1 on v0

--- a/solution.py
+++ b/solution.py
@@ -214,7 +214,10 @@
             up_bias_grad,
         ]
     )
-    summed = lax.psum(
+    build_yards = lambda my_data, axis_id, mesh_name: jax.lax.psum(
+        jax.lax.psum(my_data, axis_id), mesh_name
+    )
+    summed = build_yards(
         (
             query_grad_full,
             key_grad_full,
@@ -224,7 +227,8 @@
             down_grad_full,
             vectors,
         ),
-        ("dp", "row"),
+        "row",
+        "dp",
     )
     row_index = lax.axis_index("row")
     query_grad = lax.dynamic_slice_in_dim(

time: 1250 us -> 1420 us (1.14)
  waiting for transfers between devices: 749 us -> 932 us
    psum x1 -> x2, waiting for transfers between devices: 378 us -> 633 us  [the longest x1 415 us: local(): jax.lax.psum(my_data, axis_id)]
    reduce_scatter x2, waiting for transfers between devices: 125 us -> 54.5 us  [scatter_partial(): return lax.psum_scatter(values, 'col', scatter_dimension=1, tiled=True)]
    psum x1 -> x2, blocking collectives: 37.3 us -> 27.8 us  [the longest x1 17.6 us: local(): jax.lax.psum(my_data, axis_id)]
  transfers between devices with their start and end apart: 11 -> 12, of which waited for: 9 -> 9; matrix products, arithmetic and copies ran while one was open for 7% -> 7% of each run, Pallas kernels for 0% -> 0%
where the time goes in v1:
time: 1420 us
  waiting for transfers between devices  932 us (66%)
  matrix products  177 us (12%)
  blocking collectives  138 us (10%)
  local copies, waits for them, and re-layouts  91.6 us (6%)
  other arithmetic  59.4 us (4%)
  between operations  16.1 us (1%)
    psum x1, waiting for transfers between devices, local(): jax.lax.psum(my_data, axis_id)  415 us
    psum x1, waiting for transfers between devices, local(): jax.lax.psum(jax.lax.psum(my_data, axis_id), mesh_name)  218 us
    reduce_scatter x1, waiting for transfers between devices, local(): lax.psum_scatter(matmul(attended, out_full), 'col', scatter_dimension=1,...  78.4 us
    all_gather x2, waiting for transfers between devices, gather_grads(): return lax.all_gather(values, 'col', axis=1, tiled=True)  56.6 us
    reduce_scatter x2, waiting for transfers between devices, scatter_partial(): return lax.psum_scatter(values, 'col', scatter_dimension=1, tiled=True)  54.5 us
    dot_general x6, matrix products, matmul_nt(): lax.dot_general(left_side, right_side, (((1,), (1,)), ((), ())), preferre...  53.3 us
    psum x4, blocking collectives, feature_totals(): lax.psum((jnp.sum(first, axis=1, keepdims=True), jnp.sum(second, axis=1,...  46.8 us
    dot_general x6, matrix products, matmul(): return jnp.dot(left_side, right_side, preferred_element_type=jnp.float32)  38.8 us
  transfers between devices with their start and end apart: 12, of which 9 were waited for; matrix products, arithmetic and copies ran while one was open for 7% of the time, Pallas kernels for 0%

profile of v1, /device:TPU:0, one launch (start us, length us, event | category | flops | bytes accessed | tf_op | source)
XLA Modules:
  0.0 1415.3 jit_solution(9197477079363353562)
XLA Ops:
  10.2 12.9 all-reduce.3
  27.2 15.0 %all_gather.31 = bf16[1024,256]{1,0:T(8,128)(2,1)S(1)} all-gather(bf16[256,256]{1,0:T(8,128)(2,1)S(1)} %copy-done.27), channel_id=1, replica_groups=mesh['dp'=2,'row'=4,'col'=4] {'row'}, dimensions={0}, use_global_device_ids=true | all-gather | bytes 655360 | tf_op jit(solution)/shard_map/all_gather | solution.py:135
  42.2 17.4 %all_gather.32 = bf16[1024,256]{1,0:T(8,128)(2,1)S(1)} all-gather(bf16[256,256]{1,0:T(8,128)(2,1)S(1)} %copy-done.28), channel_id=1, replica_groups=mesh['dp'=2,'row'=4,'col'=4] {'row'}, dimensions={0}, use_global_device_ids=true | all-gather | bytes 655360 | tf_op jit(solution)/shard_map/all_gather | solution.py:133
  59.7 14.8 %all_gather.33 = bf16[1024,256]{1,0:T(8,128)(2,1)S(1)} all-gather(bf16[256,256]{1,0:T(8,128)(2,1)S(1)} %copy-done.29), channel_id=1, replica_groups=mesh['dp'=2,'row'=4,'col'=4] {'row'}, dimensions={0}, use_global_device_ids=true | all-gather | bytes 655360 | tf_op jit(solution)/shard_map/all_gather | solution.py:134
  74.5 15.8 %all_gather.34 = bf16[256,1024]{1,0:T(8,128)(2,1)} all-gather(bf16[256,256]{1,0:T(8,128)(2,1)S(1)} %copy-done.30), channel_id=1, replica_groups=mesh['dp'=2,'row'=4,'col'=4] {'row'}, dimensions={1}, use_global_device_ids=true | all-gather | bytes 655360 | tf_op jit(solution)/shard_map/all_gather | solution.py:136
  121.6 23.7 %while.26 = (s32[]{:T(128)}, bf16[4,577,4,64]{1,3,2,0:T(8,128)(2,1)}, f32[4,4,577,1]{2,1,3,0:T(4,128)}, bf16[4,577,4,64]{1,3,2,0:T(8,128)(2,1)}, bf16[4,577,4,64...) while((s32[]{:T(128)}, bf16[4,577,4,64]{1,3,2,0:T(8,128)(2,1)}, ...), condition=%wide.region_7.8_spmd, body=%wide.region_4.7_spmd.sunk | while | flops 353050112 | bytes 17368812 | solution.py:148
  153.4 6.3 fusion.82
  160.4 78.4 %reduce-scatter.5.cloned.1.call-done = f32[2308,256]{1,0:T(8,128)} async-done(((f32[2308,1024]{1,0:T(8,128)}), f32[2308,256]{1,0:T(8,128)}) %reduce-scatter.5.cloned.1.call-update) | async-done | bytes 2363408 | tf_op jit(solution)/shard_map/reduce_scatter | solution.py:151
  241.3 10.2 all-reduce.2
  256.5 37.3 %all-gather.9.cloned.1.call-done = bf16[2308,1024]{1,0:T(8,128)(2,1)} async-done(((bf16[2308,256]{1,0:T(8,128)(2,1)}), bf16[2308,1024]{1,0:T(8,128)(2,1)}) %all-gather.9.cloned.1.call-update) | async-done | bytes 4726800 | tf_op jit(solution)/shard_map/all_gather | solution.py:34
  293.7 10.1 fusion.83
  303.8 37.5 %all-gather.13.cloned.1.call-done = bf16[1024,1024]{1,0:T(8,128)(2,1)} async-done(((bf16[1024,256]{1,0:T(8,128)(2,1)}), bf16[1024,1024]{1,0:T(8,128)(2,1)}) %all-gather.13.cloned.1.call-update) | async-done | bytes 2097168 | tf_op jit(solution)/shard_map/all_gather | solution.py:138
  341.3 37.8 %all-gather.15.cloned.1.call-done = bf16[2308,1024]{1,0:T(8,128)(2,1)} async-done(((bf16[2308,256]{1,0:T(8,128)(2,1)}), bf16[2308,1024]{1,0:T(8,128)(2,1)}) %all-gather.15.cloned.1.call-update) | async-done | bytes 4726800 | tf_op jit(solution)/shard_map/all_gather | solution.py:38
  379.1 32.0 %convert_reduce_fusion = (f32[1024]{0:T(1024)}, bf16[2308,1024]{1,0:T(8,128)(2,1)S(1)}, f32[2308,1024]{1,0:T(8,128)}) fusion(f32[2308,1024]{1,0:T(8,128)} %fusion.83, f32[1024]{0:T(1024)S(1)} %copy-done.34, bf16[2308,1024]{1,0:T(8,128)(2,1)} %all-gather.15.cloned.1.call-done, bf16[1024,1024]{1,0:T(8,128)(2,1)} %all-gather.13.cloned.1.call-done), kind=kOutput, calls=%fused_computation.62 | convolution fusion | flops 5017480192 | bytes 30466048 | tf_op jit(solution)/shard_map/dot_general | solution.py:22
  413.3 8.0 fusion.84
  421.8 13.0 multiply_convert_fusion.1
  434.8 10.0 convolution_convert_fusion
  444.9 54.5 %reduce-scatter.9.cloned.1.call-done = f32[2308,256]{1,0:T(8,128)} async-done(((f32[2308,1024]{1,0:T(8,128)}), f32[2308,256]{1,0:T(8,128)}) %reduce-scatter.9.cloned.1.call-update) | async-done | bytes 2363408 | tf_op jit(solution)/shard_map/reduce_scatter | solution.py:42
  503.6 11.4 all-reduce.1
  516.4 33.3 %reduce-scatter.7.cloned.1.call-done = bf16[2308,256]{1,0:T(8,128)(2,1)} async-done(((bf16[2308,1024]{1,0:T(8,128)(2,1)}), bf16[2308,256]{1,0:T(8,128)(2,1)}) %reduce-scatter.7.cloned.1.call-update) | async-done | bytes 1181712 | tf_op jit(solution)/shard_map/reduce_scatter | solution.py:161
  549.7 6.5 convert_reduce_fusion.5
  556.3 10.4 fusion.91
  566.8 8.9 fusion.92
  575.7 18.9 %all-gather.17.cloned.1.call-done = bf16[2308,1024]{1,0:T(8,128)(2,1)} async-done(((bf16[2308,256]{1,0:T(8,128)(2,1)}), bf16[2308,1024]{1,0:T(8,128)(2,1)}) %all-gather.17.cloned.1.call-update) | async-done | bytes 4726800 | tf_op jit(solution)/shard_map/all_gather | solution.py:38
  608.9 43.5 %while.27 = (s32[]{:T(128)}, bf16[4,577,4,64]{1,3,2,0:T(8,128)(2,1)}, bf16[4,577,4,64]{1,3,2,0:T(8,128)(2,1)}, bf16[4,577,4,64]{1,3,2,0:T(8,128)(2,1)}, bf16[4,5...) while((s32[]{:T(128)}, ...), condition=%wide.region_21.22_spmd, body=%wide.region_19.21_spmd.sunk | while | flops 869015040 | bytes 49986844 | solution.py:184
  672.3 5.4 fusion.90
  691.4 5.1 add_add_fusion
  696.9 415.2 %all-reduce.9.cloned.1.call-done = (f32[1024,256]{1,0:T(8,128)}, f32[1024,256]{1,0:T(8,128)}, f32[1024,256]{1,0:T(8,128)}, f32[256,1024]{1,0:T(8,128)}, f32[1024,1024]{1,0:T(8,128)}, /*index=5*/f32[1024,1024]{1,0:T(8,128)}) async-done(((f32[1024,256]{1,0:T(8,128)}, f32[1024,256]{1,0:T(8,128)}, f32[1024,256]{1,0:T(8,128)}, f32[256,1024]{1,0:T(8,128)}, f32[1024,1024]{1,0:T(8,128)}, ...) | async-done | bytes 12582928 | tf_op jit(solution)/shard_map/psum | solution.py:218
  1132.1 17.6 %psum.168 = f32[3072]{0:T(1024)} all-reduce(f32[3072]{0:T(1024)} %constant_dynamic-update-slice_fusion), channel_id=1, replica_groups=mesh['dp'=2,'row'=4,'col'=4] {'row'}, use_global_device_ids=true, to_apply=%region_42.43 | all-reduce | flops 3072 | bytes 24576 | tf_op jit(solution)/shard_map/psum | solution.py:218
  1149.7 10.1 psum.169
  1162.4 12.2 all-reduce
  1181.9 217.7 %all-reduce.11.cloned.1.call-done = (f32[1024,256]{1,0:T(8,128)}, f32[1024,256]{1,0:T(8,128)}, f32[1024,256]{1,0:T(8,128)}, f32[256,1024]{1,0:T(8,128)}, f32[1024,1024]{1,0:T(8,128)}, /*index=5*/f32[1024,1024]{1,0:T(8,128)}) async-done(((f32[1024,256]{1,0:T(8,128)}, f32[1024,256]{1,0:T(8,128)}, f32[1024,256]{1,0:T(8,128)}, f32[256,1024]{1,0:T(8,128)}, f32[1024,1024]{1,0:T(8,128)}, ...) | async-done | bytes 12582928 | tf_op jit(solution)/shard_map/psum | solution.py:217
  (231 shorter events, 214.9 us)
Async XLA Ops:
  8.0 19.1 %copy-start.27 = (bf16[256,256]{1,0:T(8,128)(2,1)S(1)}, bf16[256,256]{1,0:T(8,128)(2,1)}, u32[]{:S(2)}) copy-start(bf16[256,256]{1,0:T(8,128)(2,1)} %param.24) | copy-start | bytes 393220
  8.0 34.2 %copy-start.28 = (bf16[256,256]{1,0:T(8,128)(2,1)S(1)}, bf16[256,256]{1,0:T(8,128)(2,1)}, u32[]{:S(2)}) copy-start(bf16[256,256]{1,0:T(8,128)(2,1)} %param.22) | copy-start | bytes 393220
  8.0 51.6 %copy-start.29 = (bf16[256,256]{1,0:T(8,128)(2,1)S(1)}, bf16[256,256]{1,0:T(8,128)(2,1)}, u32[]{:S(2)}) copy-start(bf16[256,256]{1,0:T(8,128)(2,1)} %param.23) | copy-start | bytes 393220
  8.1 82.2 %all-gather.7.cloned.1.call-start = ((), (), s32[]{:S(2)}) async-start(), calls=%async_computation.4 | async-start | bytes 5918720 | tf_op jit(solution)/shard_map/all_gather | solution.py:34
  10.2 64.3 %copy-start.30 = (bf16[256,256]{1,0:T(8,128)(2,1)S(1)}, bf16[256,256]{1,0:T(8,128)(2,1)}, u32[]{:S(2)}) copy-start(bf16[256,256]{1,0:T(8,128)(2,1)} %param.27) | copy-start | bytes 393220
  23.9 66.4 %copy-start.36 = (f32[256]{0:T(256)S(1)}, f32[256]{0:T(256)}, u32[]{:S(2)}) copy-start(f32[256]{0:T(256)} %param.26) | copy-start | bytes 3076
  27.1 211.7 %reduce-scatter.5.cloned.1.call-start = ((), (), s32[]{:S(2)}) async-start(), calls=%async_computation.5 | async-start | bytes 11837440 | tf_op jit(solution)/shard_map/reduce_scatter | solution.py:151
  42.2 48.0 %copy-start.15 = (bf16[1024,256]{1,0:T(8,128)(2,1)}, bf16[1024,256]{1,0:T(8,128)(2,1)S(1)}, u32[]{:S(2)}) copy-start(bf16[1024,256]{1,0:T(8,128)(2,1)S(1)} %all_gather.31) | copy-start | bytes 1572868
  59.7 42.1 %copy-start.17 = (bf16[1024,256]{1,0:T(8,128)(2,1)}, bf16[1024,256]{1,0:T(8,128)(2,1)S(1)}, u32[]{:S(2)}) copy-start(bf16[1024,256]{1,0:T(8,128)(2,1)S(1)} %all_gather.32) | copy-start | bytes 1572868
  74.5 36.6 %copy-start.19 = (bf16[1024,256]{1,0:T(8,128)(2,1)}, bf16[1024,256]{1,0:T(8,128)(2,1)S(1)}, u32[]{:S(2)}) copy-start(bf16[1024,256]{1,0:T(8,128)(2,1)S(1)} %all_gather.33) | copy-start | bytes 1572868
  145.3 14.4 %copy-start.2 = (bf16[4,577,4,64]{1,3,2,0:T(8,128)(2,1)}, bf16[4,577,4,64]{1,3,2,0:T(8,128)(2,1)S(1)}, u32[]{:S(2)}) copy-start(bf16[4,577,4,64]{1,3,2,0:T(8,128)(2,1)S(1)} %get-tuple-element.416) | copy-start | bytes 3545092
  145.3 14.4 %copy-start.4 = (bf16[4,577,4,64]{1,3,2,0:T(8,128)(2,1)}, bf16[4,577,4,64]{1,3,2,0:T(8,128)(2,1)S(1)}, u32[]{:S(2)}) copy-start(bf16[4,577,4,64]{1,3,2,0:T(8,128)(2,1)S(1)} %get-tuple-element.417) | copy-start | bytes 3545092
  159.7 79.1 %copy-start = (bf16[2308,256]{1,0:T(8,128)(2,1)S(1)}, bf16[2308,256]{1,0:T(8,128)(2,1)}, u32[]{:S(2)}) copy-start(bf16[2308,256]{1,0:T(8,128)(2,1)} %param.21) | copy-start | bytes 3545092
  159.8 96.7 %all-gather.11.cloned.1.call-start = ((), (), s32[]{:S(2)}) async-start(), calls=%async_computation.7 | async-start | bytes 2621440 | tf_op jit(solution)/shard_map/all_gather | solution.py:137
  160.3 91.9 %copy-start.32 = (f32[256]{0:T(256)S(1)}, f32[256]{0:T(256)}, u32[]{:S(2)}) copy-start(f32[256]{0:T(256)} %param.35) | copy-start | bytes 3076
  160.3 133.4 %all-gather.9.cloned.1.call-start = ((), (), s32[]{:S(2)}) async-start(), calls=%async_computation.6 | async-start | bytes 5918720 | tf_op jit(solution)/shard_map/all_gather | solution.py:34
  255.0 86.3 %all-gather.13.cloned.1.call-start = ((), (), s32[]{:S(2)}) async-start(), calls=%async_computation.8 | async-start | bytes 2621440 | tf_op jit(solution)/shard_map/all_gather | solution.py:138
  255.6 123.5 %all-gather.15.cloned.1.call-start = ((), (), s32[]{:S(2)}) async-start(), calls=%async_computation.10 | async-start | bytes 5918720 | tf_op jit(solution)/shard_map/all_gather | solution.py:38
  256.4 122.8 %copy-start.34 = (f32[1024]{0:T(1024)S(1)}, f32[1024]{0:T(1024)}, u32[]{:S(2)}) copy-start(f32[1024]{0:T(1024)} %param.30) | copy-start | bytes 12292
  256.4 243.0 %reduce-scatter.9.cloned.1.call-start = ((), (), s32[]{:S(2)}) async-start(), calls=%async_computation.11 | async-start | bytes 11837440 | tf_op jit(solution)/shard_map/reduce_scatter | solution.py:42
  379.1 34.2 %copy-start.35 = (bf16[1024,1024]{1,0:T(8,128)(2,1)S(1)}, bf16[1024,1024]{1,0:T(8,128)(2,1)}, u32[]{:S(2)}) copy-start(bf16[1024,1024]{1,0:T(8,128)(2,1)} %all-gather.11.cloned.1.call-done) | copy-start | bytes 6291460
  421.4 128.4 %reduce-scatter.7.cloned.1.call-start = ((), (), s32[]{:S(2)}) async-start(), calls=%async_computation.9 | async-start | bytes 5918720 | tf_op jit(solution)/shard_map/reduce_scatter | solution.py:161
  444.8 104.9 %copy-start.14 = (bf16[2308,256]{1,0:T(8,128)(2,1)S(1)}, bf16[2308,256]{1,0:T(8,128)(2,1)}, u32[]{:S(2)}) copy-start(bf16[2308,256]{1,0:T(8,128)(2,1)} %param.37) | copy-start | bytes 3545092
  444.8 149.7 %all-gather.17.cloned.1.call-start = ((), (), s32[]{:S(2)}) async-start(), calls=%async_computation.12 | async-start | bytes 5918720 | tf_op jit(solution)/shard_map/all_gather | solution.py:38
  556.2 10.5 slice-start
  556.3 555.8 %all-reduce.9.cloned.1.call-start = ((), (), s32[]{:S(2)}) async-start(), calls=%async_computation.14 | async-start | bytes 25165824 | tf_op jit(solution)/shard_map/psum | solution.py:218
  566.8 27.8 %copy-start.22 = (bf16[256,1024]{1,0:T(8,128)(2,1)S(1)}, bf16[256,1024]{1,0:T(8,128)(2,1)}, u32[]{:S(2)}) copy-start(bf16[256,1024]{1,0:T(8,128)(2,1)} %all_gather.34) | copy-start | bytes 1572868
  665.1 12.6 slice-start.2
  685.9 436.7 %reduce-scatter.11.cloned.1.call-start = ((), (), s32[]{:S(2)}) async-start(), calls=%async_computation.13 | async-start | bytes 11837440 | tf_op jit(solution)/shard_map/reduce_scatter | solution.py:42
  696.6 703.0 %all-reduce.11.cloned.1.call-start = ((), (), s32[]{:S(2)}) async-start(), calls=%async_computation.15 | async-start | bytes 25165824 | tf_op jit(solution)/shard_map/psum | solution.py:217
  1112.0 10.5 copy-start.31
  1114.5 62.2 %copy-start.8 = (f32[2308,256]{1,0:T(8,128)S(1)}, f32[2308,256]{1,0:T(8,128)}, u32[]{:S(2)}) copy-start(f32[2308,256]{1,0:T(8,128)} %get-tuple-element.205) | copy-start | bytes 7090180
  (26 other events, 107.2 us)
Sparse Core Ops, SparseCore 0:
  27.2 38.4 all-gather.6
  159.9 78.8 reduce-scatter.4
  556.4 38.1 all-gather.16
  696.7 78.0 reduce-scatter.10
  1112.2 287.3 all-reduce.10
Sparse Core Ops, SparseCore 1:
  161.8 46.4 all-gather.10
  255.1 38.5 all-gather.8
  295.2 46.1 all-gather.12
  342.9 36.2 all-gather.14
  421.4 77.8 reduce-scatter.8
  501.9 47.8 reduce-scatter.6
  686.0 426.0 all-reduce.8
